TPU v7x, 128 devices: a whole 4x4x4 slice. The times are simulated.
128 devices in a mesh: ctx: 16 (over z_hi, x, core), head: 8 (over z_lo, y).
Axes of the slice: x: 4, y: 4, z: 4 (z_hi: 2, z_lo: 2; z = z_hi * 2 + z_lo), core: 2. Of those that a mesh axis runs over, the one named last changes fastest.
Arguments:
- tokens: bfloat16 [16384, 4096], P('ctx', 'head'), may hold values from -23 to 23
- proj_weight: bfloat16 [4096, 32, 384], P(None, 'head'), may hold values from -1 to 1
- partner_shard: int32 [32, 256, 3], P('head'), may hold values from 0 to 15, all different within a row; in each aligned block of 16 rows (0 to 15, 16 to 31, ..., all dimensions but the last counted through in order) at most 6 rows name the same one
- partner_block: int32 [32, 256, 3], P('head'), may hold values from 0 to 15
Outputs:
- attended: bfloat16 [16384, 32, 128], P('ctx', 'head')
Inputs may be any that keep to these rules, and one draw needn't show every extreme that they name: `partner_shard`: the 3 entries of one row differ. For each head, within each aligned run of 16 block rows, no value is named more than 6 times, and some runs name one value exactly 6 times.
All inputs are finite; a program needn't handle non-finite values.
Results may differ from a plain program's by a relative error of at most 0.008.
Values may be sent and summed in bfloat16 or wider, within the bound.
A program may use at most 192 MiB of HBM per device.

v0:
```python
import jax
import jax.numpy as jnp
from jax import lax
from jax.sharding import PartitionSpec as P

HEAD_DIMENSION = 128
BLK = 64
GLOB = 2
RAND = 3


def padded_2(cells, sides, width):
    for axis, dim in sides:
        count = lax.axis_size(axis)
        head = lax.slice_in_dim(cells, 0, width, axis=dim)
        tail = lax.slice_in_dim(cells, cells.shape[dim] - width, cells.shape[dim], axis=dim)
        cells = jnp.concatenate(
            [
                lax.ppermute(tail, axis, [(i, (i + 1) % count) for i in range(count)]),
                cells,
                lax.ppermute(head, axis, [((i + 1) % count, i) for i in range(count)]),
            ],
            axis=dim,
        )
    return cells


def from_root(block, axis, holder):
    block = jnp.where(lax.axis_index(axis) == holder, block, jnp.zeros_like(block))
    return lax.psum(block, axis)


def combined_all(part, axis, combine):
    gathered = jax.tree.map(lambda a: lax.all_gather(a, axis), part)

    def take(source):
        return jax.tree.map(lambda a: lax.dynamic_index_in_dim(a, source, 0, False), gathered)

    return lax.fori_loop(
        1, lax.axis_size(axis), lambda source, state: combine(state, take(source)), take(0)
    )


def per_device(tokens, proj_weight, partner_shard, partner_block):
    row_count = tokens.shape[0]
    head_count = proj_weight.shape[1]
    blocks = row_count // BLK
    shard_index = lax.axis_index("ctx")
    inverse_root_scale = HEAD_DIMENSION ** (-0.5)
    packed = jnp.einsum(
        "td,dhe->the",
        lax.all_gather(tokens, "head", axis=1, tiled=True),
        proj_weight,
        preferred_element_type=jnp.float32,
    ).astype(jnp.bfloat16)
    queries = packed[..., :HEAD_DIMENSION]
    keyval = packed[..., HEAD_DIMENSION:]
    padded = padded_2(keyval, (("ctx", 0),), BLK)
    window = jnp.concatenate(
        [
            padded[0:row_count].reshape(blocks, BLK, head_count, 2 * HEAD_DIMENSION),
            padded[BLK : row_count + BLK].reshape(blocks, BLK, head_count, 2 * HEAD_DIMENSION),
            padded[2 * BLK : row_count + 2 * BLK].reshape(
                blocks, BLK, head_count, 2 * HEAD_DIMENSION
            ),
        ],
        axis=1,
    )
    global_pack = from_root(packed[: GLOB * BLK], "ctx", 0)
    global_query = global_pack[..., :HEAD_DIMENSION]
    global_keyval = global_pack[..., HEAD_DIMENSION:]
    row_total = blocks * RAND
    owners = lax.dynamic_slice_in_dim(partner_shard, shard_index * blocks, blocks, 1).reshape(
        head_count, row_total
    )
    offsets = lax.dynamic_slice_in_dim(partner_block, shard_index * blocks, blocks, 1).reshape(
        head_count, row_total
    )
    partner_index = owners * blocks + offsets
    block_rows = lax.all_gather(keyval, "ctx", axis=0, tiled=True)
    piece_blocks = block_rows.shape[0] // BLK
    piece_hot = (partner_index[..., None] == jnp.arange(piece_blocks)).astype(jnp.bfloat16)
    blocked = block_rows.reshape(piece_blocks, BLK, head_count, 2 * HEAD_DIMENSION)
    fetched = jnp.einsum(
        "hrb,bthe->hrte", piece_hot, blocked, preferred_element_type=jnp.float32
    ).astype(jnp.bfloat16)
    remote = fetched
    remote = remote.reshape(head_count, blocks, RAND * BLK, 2 * HEAD_DIMENSION)
    blocked_query_rows = queries.reshape(blocks, BLK, head_count, HEAD_DIMENSION)
    window_scores = jnp.einsum(
        "bqhd,bkhd->bhqk",
        blocked_query_rows,
        window[..., :HEAD_DIMENSION],
        preferred_element_type=jnp.float32,
    )
    global_scores = jnp.einsum(
        "bqhd,khd->bhqk",
        blocked_query_rows,
        global_keyval[..., :HEAD_DIMENSION],
        preferred_element_type=jnp.float32,
    )
    remote_scores = jnp.einsum(
        "bqhd,hbkd->bhqk",
        blocked_query_rows,
        remote[..., :HEAD_DIMENSION],
        preferred_element_type=jnp.float32,
    )
    logit_scores = (
        jnp.concatenate([window_scores, global_scores, remote_scores], axis=-1) * inverse_root_scale
    )
    softmax_weight_matrix = jax.nn.softmax(logit_scores, axis=-1).astype(jnp.bfloat16)
    width_window = 3 * BLK
    width_global = GLOB * BLK
    context = jnp.einsum(
        "bhqk,bkhd->bqhd",
        softmax_weight_matrix[..., :width_window],
        window[..., HEAD_DIMENSION:],
        preferred_element_type=jnp.float32,
    )
    context = context + jnp.einsum(
        "bhqk,khd->bqhd",
        softmax_weight_matrix[..., width_window : width_window + width_global],
        global_keyval[..., HEAD_DIMENSION:],
        preferred_element_type=jnp.float32,
    )
    context = context + jnp.einsum(
        "bhqk,hbkd->bqhd",
        softmax_weight_matrix[..., width_window + width_global :],
        remote[..., HEAD_DIMENSION:],
        preferred_element_type=jnp.float32,
    )
    sparse_attention_output = context.astype(jnp.bfloat16).reshape(
        row_count, head_count, HEAD_DIMENSION
    )
    lead_scores = (
        jnp.einsum(
            "qhd,khd->hqk",
            global_query,
            keyval[..., :HEAD_DIMENSION],
            preferred_element_type=jnp.float32,
        )
        * inverse_root_scale
    )
    maxima = jnp.max(lead_scores, axis=-1)
    exp_terms = jnp.exp(lead_scores - maxima[..., None])
    totals = jnp.sum(exp_terms, axis=-1)
    summed = jnp.einsum(
        "hqk,khd->hqd",
        exp_terms,
        keyval[..., HEAD_DIMENSION:].astype(jnp.float32),
        precision=lax.Precision.HIGHEST,
    )

    def combine(first, second):
        max_first, total_first, sum_first = first
        max_second, total_second, sum_second = second
        larger = jnp.maximum(max_first, max_second)
        factor_first = jnp.exp(max_first - larger)
        factor_second = jnp.exp(max_second - larger)
        return (
            larger,
            total_first * factor_first + total_second * factor_second,
            sum_first * factor_first[..., None] + sum_second * factor_second[..., None],
        )

    maxima, totals, summed = combined_all((maxima, totals, summed), "ctx", combine)
    global_out = jnp.transpose((summed / totals[..., None]).astype(jnp.bfloat16), (1, 0, 2))
    head_rows = jnp.where(shard_index == 0, global_out, sparse_attention_output[: GLOB * BLK])
    return jnp.concatenate([head_rows, sparse_attention_output[GLOB * BLK :]], axis=0)


def solution(mesh):
    in_specs = (
        P("ctx", "head"),
        P(None, "head", None),
        P("head", None, None),
        P("head", None, None),
    )
    out_specs = P("ctx", "head", None)
    return jax.shard_map(
        per_device, mesh=mesh, in_specs=in_specs, out_specs=out_specs, check_vma=False
    )
```

profile of v0, /device:TPU:1, one launch (start us, length us, event | category | flops | bytes accessed | tf_op | source)
XLA Modules:
  0.0 600.8 jit_solution(12266525961735290425)
XLA Ops:
  7.3 96.7 %all-gather.9.cloned.1.call-done = bf16[1024,4096]{1,0:T(8,128)(2,1)} async-done(((bf16[1024,512]{1,0:T(8,128)(2,1)}), bf16[1024,4096]{1,0:T(8,128)(2,1)}) %all-gather.9.cloned.1.call-update) | async-done | bytes 8388624 | tf_op jit(solution)/shard_map/all_gather | solution.py:52
  104.0 18.3 %fusion.22 = bf16[1024,4,384]{2,0,1:T(8,128)(2,1)S(1)} fusion(bf16[4096,4,384]{2,1,0:T(4,128)(2,1)} %param.7, bf16[1024,4096]{1,0:T(8,128)(2,1)} %all-gather.9.cloned.1.call-done), kind=kOutput, calls=%fused_computation.29 | convolution fusion | flops 12886474752 | bytes 24117248 | tf_op jit(solution)/shard_map/td,dhe->the/dot_general | solution.py:50
  123.2 138.2 %all-reduce.2.cloned.1.call-done = bf16[128,4,384]{2,0,1:T(8,128)(2,1)} async-done(((bf16[128,4,384]{2,0,1:T(8,128)(2,1)}), bf16[128,4,384]{2,0,1:T(8,128)(2,1)}) %all-reduce.2.cloned.1.call-update) | async-done | bytes 393232 | tf_op jit(solution)/shard_map/psum | solution.py:30
  261.4 1.4 multiply_reduce_fusion
  262.8 1.3 copy-done.1
  264.1 2.2 fusion.30
  266.4 1.5 slice.118
  267.9 1.8 fusion.56
  271.3 1.3 slice.116
  272.6 1.4 collective-permute-done.1
  274.4 5.0 pad_maximum_fusion
  279.4 3.4 fusion.54
  282.8 4.1 fusion.20
  286.9 25.5 %all-gather.3 = f32[16,4,128]{2,1,0:T(4,128)S(1)} all-gather(f32[1,4,128]{2,1,0:T(4,128)S(1)} %bitcast.75), channel_id=2, replica_groups=mesh['ctx'=16,'head'=8] {'ctx'}, dimensions={0}, use_global_device_ids=true | all-gather | bytes 34816 | tf_op jit(solution)/shard_map/all_gather | solution.py:34
  312.9 19.5 %all-gather.4 = f32[16,4,128]{2,1,0:T(4,128)S(1)} all-gather(f32[1,4,128]{2,1,0:T(4,128)S(1)} %bitcast.76), channel_id=3, replica_groups=mesh['ctx'=16,'head'=8] {'ctx'}, dimensions={0}, use_global_device_ids=true | all-gather | bytes 34816 | tf_op jit(solution)/shard_map/all_gather | solution.py:34
  332.4 1.3 convolution_bitcast_fusion
  334.8 19.0 %while.19 = (s32[]{:T(128)}, f32[4,128]{1,0:T(4,128)S(1)}, f32[4,128]{1,0:T(4,128)S(1)}, f32[4,128,128]{2,1,0:T(8,128)S(1)}, f32[16,4,128]{2,1,0:T(4,128)S(1)}, ...) while((s32[]{:T(128)}, f32[4,128]{1,0:T(4,128)S(1)}, ...), condition=%wide.region_4.5_spmd, body=%wide.region_3.4_spmd.sunk | while | flops 199685 | bytes 807063 | solution.py:39
  334.8 1.3 fusion.61
  336.1 1.2 fusion.61
  337.4 1.2 fusion.61
  338.7 1.3 fusion.61
  353.8 158.4 %all-gather.11.cloned.1.call-done = bf16[16384,4,256]{2,0,1:T(8,128)(2,1)} async-done(((bf16[1024,4,256]{2,0,1:T(8,128)(2,1)}), bf16[16384,4,256]{2,0,1:T(8,128)(2,1)}) %all-gather.11.cloned.1.call-update) | async-done | bytes 33554448 | tf_op jit(solution)/shard_map/all_gather | solution.py:80
  512.2 34.4 %fusion.11 = bf16[4,48,64,256]{3,1,2,0:T(8,128)(2,1)S(1)} fusion(bf16[256,64,4,256]{3,1,0,2:T(8,128)(2,1)} %bitcast.65, s32[4,48]{1,0:T(4,128)S(1)} %add.84), kind=kOutput, calls=%fused_computation.20 | convolution fusion | flops 1613807616 | bytes 39846656 | tf_op jit(solution)/shard_map/hrb,bthe->hrte/dot_general | solution.py:84
  546.6 2.5 copy.42
  549.1 1.8 fusion.55
  550.9 4.1 fusion.18
  555.0 28.1 %fusion.57 = (f32[16,4,64]{2,1,0:T(4,128)S(1)}, f32[16,4,64,512]{3,2,1,0:T(8,128)}) fusion(f32[16,4,64,192]{3,2,1,0:T(8,128)} %fusion.18, f32[16,4,64,128]{3,2,1,0:T(8,128)S(1)} %convolution_bitcast_fusion, f32[16,4,64,192]{3,2,1,0:T(8,128)S(1)} %copy-done.5), kind=kOutput, calls=%fused_computation.71 | output fusion | flops 10486271 | bytes 16793600 | tf_op jit(solution)/shard_map/sub | solution.py:111
  583.1 4.1 divide_convert_fusion
  587.1 1.3 fusion.14
  588.4 1.6 fusion.36
  590.4 1.4 fusion.29
  592.2 1.8 copy.48
  (64 shorter events, 19.6 us)
Async XLA Ops:
  6.5 97.4 %all-gather.9.cloned.1.call-start = ((), (), s32[]{:S(2)}) async-start(), calls=%async_computation | async-start | bytes 9437184 | tf_op jit(solution)/shard_map/all_gather | solution.py:52
  7.3 254.2 %all-reduce.2.cloned.1.call-start = ((), (), s32[]{:S(2)}) async-start(), calls=%async_computation.1 | async-start | bytes 786432 | tf_op jit(solution)/shard_map/psum | solution.py:30
  122.3 144.1 %copy-start.4 = (bf16[1024,4,384]{2,0,1:T(8,128)(2,1)}, bf16[1024,4,384]{2,0,1:T(8,128)(2,1)S(1)}, u32[]{:S(2)}) copy-start(bf16[1024,4,384]{2,0,1:T(8,128)(2,1)S(1)} %fusion.22) | copy-start | bytes 9437188
  123.2 210.6 %all-gather.13.cloned.1.call-start = ((), (), s32[]{:S(2)}) async-start(), calls=%async_computation.3 | async-start | bytes 4456448 | tf_op jit(solution)/shard_map/all_gather | solution.py:34
  262.8 1.3 copy-start.1
  266.3 245.9 %all-gather.11.cloned.1.call-start = ((), (), s32[]{:S(2)}) async-start(), calls=%async_computation.2 | async-start | bytes 35651584 | tf_op jit(solution)/shard_map/all_gather | solution.py:80
  267.9 6.2 %copy-start = (bf16[1024,4,256]{2,0,1:T(8,128)(2,1)S(1)}, bf16[1024,4,256]{2,0,1:T(8,128)(2,1)}, u32[]{:S(2)}) copy-start(bf16[1024,4,256]{2,0,1:T(8,128)(2,1)} %slice.118) | copy-start | bytes 6291460
  269.7 2.9 collective-permute-start
  269.7 4.4 collective-permute-start.1
  282.8 29.6 %copy-start.2 = (f32[4,128,1024]{2,1,0:T(8,128)S(1)}, f32[4,128,1024]{2,1,0:T(8,128)}, u32[]{:S(2)}) copy-start(f32[4,128,1024]{2,1,0:T(8,128)} %copy-done.1) | copy-start | bytes 6291460
  550.9 4.1 copy-start.5
  588.4 2.0 copy-start.3
Sparse Core Ops, SparseCore 0:
  9.0 94.9 all-gather.8
  123.3 138.0 all-reduce.1
  266.4 57.4 all-gather.12
  326.3 185.8 all-gather.10
where the time goes:
time: 610 us; the launch traced here: 601 us
  waiting for transfers between devices  396 us (65%)
  matrix products  70 us (11%)
  other arithmetic  58.3 us (10%)
  blocking collectives  45 us (7%)
  local copies, waits for them, and re-layouts  17.1 us (3%)
  between operations  13.6 us (2%)
    all_gather x1, waiting for transfers between devices, per_device(): block_rows = lax.all_gather(keyval, 'ctx', axis=0, tiled=True)  158 us
    psum x1, waiting for transfers between devices, from_root(): return lax.psum(block, axis)  138 us
    all_gather x1, waiting for transfers between devices, per_device(): lax.all_gather(tokens, 'head', axis=1, tiled=True)  96.7 us
    all_gather x2, blocking collectives, combined_all(): gathered = jax.tree.map(lambda a: lax.all_gather(a, axis), part)  45 us
    dot_general x1, matrix products, per_device(): jnp.einsum('hrb,bthe->hrte', piece_hot, blocked, preferred_element_type=j...  34.4 us
    sub x1, other arithmetic, per_device(): jax.nn.softmax(logit_scores, axis=-1).astype(jnp.bfloat16)  28.1 us
    dot_general x1, matrix products, per_device(): jnp.einsum('td,dhe->the', lax.all_gather(tokens, 'head', axis=1, tiled=Tr...  18.3 us
    add x15, other arithmetic, combine(): sum_first * factor_first[..., None] + sum_second * factor_second[..., None]  18.2 us
  transfers between devices with their start and end apart: 6, of which 4 were waited for; matrix products, arithmetic and copies ran while one was open for 7% of the time, Pallas kernels for 0%

commit v1 on v0

--- a/solution.py
+++ b/solution.py
@@ -77,7 +77,9 @@
         head_count, row_total
     )
     partner_index = owners * blocks + offsets
-    block_rows = lax.all_gather(keyval, "ctx", axis=0, tiled=True)
+    block_rows = jnp.concatenate(
+        lax.all_to_all(jnp.stack([keyval] * lax.axis_size("ctx")), "ctx", 0, 0), axis=0
+    )
     piece_blocks = block_rows.shape[0] // BLK
     piece_hot = (partner_index[..., None] == jnp.arange(piece_blocks)).astype(jnp.bfloat16)
     blocked = block_rows.reshape(piece_blocks, BLK, head_count, 2 * HEAD_DIMENSION)

time: 610 us -> 799 us (1.31)
  waiting for transfers between devices: 396 us -> 546 us
  local copies, waits for them, and re-layouts: 17.1 us -> 51.4 us
    ppermute x1, waiting for transfers between devices: 0.01 us -> 171 us  [padded_2(): lax.ppermute(tail, axis, [(i, (i + 1) % count) for i in range(count)])]
    all_gather x1 -> x0, waiting for transfers between devices: 158 us -> none  [per_device(): block_rows = lax.all_gather(keyval, 'ctx', axis=0, tiled=True)]
    psum x1, waiting for transfers between devices: 138 us -> 278 us  [from_root(): return lax.psum(block, axis)]
    all_to_all x0 -> x1, local copies, waits for them, and re-layouts: none -> 22.9 us  [per_device(): lax.all_to_all(jnp.stack([keyval] * lax.axis_size('ctx')), 'ctx', 0, 0)]
    another operation x0 -> x1, local copies, waits for them, and re-layouts: none -> 11 us  [per_device(): jnp.stack([keyval] * lax.axis_size('ctx'))]
  transfers between devices with their start and end apart: 6 -> 6, of which waited for: 4 -> 3; matrix products, arithmetic and copies ran while one was open for 7% -> 6% of each run, Pallas kernels for 0% -> 0%
where the time goes in v1:
time: 799 us; the launch traced here: 793 us
  waiting for transfers between devices  546 us (68%)
  matrix products  71.7 us (9%)
  other arithmetic  58.5 us (7%)
  local copies, waits for them, and re-layouts  51.4 us (6%)
  blocking collectives  42.3 us (5%)
  between operations  13.6 us (2%)
  starting transfers between devices  8.42 us (1%)
    psum x1, waiting for transfers between devices, from_root(): return lax.psum(block, axis)  278 us
    ppermute x1, waiting for transfers between devices, padded_2(): lax.ppermute(tail, axis, [(i, (i + 1) % count) for i in range(count)])  171 us
    all_gather x1, waiting for transfers between devices, per_device(): lax.all_gather(tokens, 'head', axis=1, tiled=True)  96.7 us
    all_gather x2, blocking collectives, combined_all(): gathered = jax.tree.map(lambda a: lax.all_gather(a, axis), part)  42.3 us
    dot_general x1, matrix products, per_device(): jnp.einsum('hrb,bthe->hrte', piece_hot, blocked, preferred_element_type=j...  34.4 us
    sub x1, other arithmetic, per_device(): jax.nn.softmax(logit_scores, axis=-1).astype(jnp.bfloat16)  28.1 us
    all_to_all x1, local copies, waits for them, and re-layouts, per_device(): lax.all_to_all(jnp.stack([keyval] * lax.axis_size('ctx')), 'ctx', 0, 0)  22.9 us
    dot_general x1, matrix products, per_device(): jnp.einsum('td,dhe->the', lax.all_gather(tokens, 'head', axis=1, tiled=Tr...  18.3 us
  transfers between devices with their start and end apart: 6, of which 3 were waited for; matrix products, arithmetic and copies ran while one was open for 6% of the time, Pallas kernels for 0%

profile of v1, /device:TPU:1, one launch (start us, length us, event | category | flops | bytes accessed | tf_op | source)
XLA Modules:
  0.0 792.7 jit_solution(3771661223384916965)
XLA Ops:
  7.3 96.7 %all-gather.8.cloned.1.call-done = bf16[1024,4096]{1,0:T(8,128)(2,1)} async-done(((bf16[1024,512]{1,0:T(8,128)(2,1)}), bf16[1024,4096]{1,0:T(8,128)(2,1)}) %all-gather.8.cloned.1.call-update) | async-done | bytes 8388624 | tf_op jit(solution)/shard_map/all_gather | solution.py:52
  104.0 18.3 %fusion.22 = bf16[1024,4,384]{2,0,1:T(8,128)(2,1)S(1)} fusion(bf16[4096,4,384]{2,1,0:T(4,128)(2,1)} %param.7, bf16[1024,4096]{1,0:T(8,128)(2,1)} %all-gather.8.cloned.1.call-done), kind=kOutput, calls=%fused_computation.29 | convolution fusion | flops 12886474752 | bytes 24117248 | tf_op jit(solution)/shard_map/td,dhe->the/dot_general | solution.py:50
  122.3 1.7 copy-done.3
  124.1 11.0 %stack.2 = bf16[16,1024,4,256]{3,1,2,0:T(8,128)(2,1)} broadcast(bf16[1024,4,256]{2,0,1:T(8,128)(2,1)S(1)} %slice.118), dimensions={1,2,3} | broadcast | bytes 35651584 | tf_op jit(solution)/shard_map/stack | solution.py:81
  135.1 7.4 all-to-all-start
  142.6 1.8 slice_select_fusion
  144.5 277.9 %all-reduce.2.cloned.1.call-done = bf16[128,4,384]{2,0,1:T(8,128)(2,1)} async-done(((bf16[128,4,384]{2,0,1:T(8,128)(2,1)}), bf16[128,4,384]{2,0,1:T(8,128)(2,1)}) %all-reduce.2.cloned.1.call-update) | async-done | bytes 393232 | tf_op jit(solution)/shard_map/psum | solution.py:30
  422.3 1.8 multiply_reduce_fusion
  424.2 1.5 copy-done
  425.7 3.4 fusion.30
  429.1 1.6 fusion.56
  432.0 1.3 slice.116
  433.3 171.1 %collective-permute-done = bf16[64,4,256]{2,0,1:T(8,128)(2,1)S(1)} collective-permute-done((bf16[64,4,256]{2,0,1:T(8,128)(2,1)}, bf16[64,4,256]{2,0,1:T(8,128)(2,1)S(1)}, u32[]{:S(2)}, u32[]{:S(2)}) %collective-permute-start) | collective-permute-done | bytes 131104 | tf_op jit(solution)/shard_map/ppermute | solution.py:19
  604.7 5.0 pad_maximum_fusion
  609.7 3.4 fusion.54
  613.1 4.1 fusion.20
  617.2 22.4 %all-gather.3 = f32[16,4,128]{2,1,0:T(4,128)S(1)} all-gather(f32[1,4,128]{2,1,0:T(4,128)S(1)} %bitcast.75), channel_id=2, replica_groups=mesh['ctx'=16,'head'=8] {'ctx'}, dimensions={0}, use_global_device_ids=true | all-gather | bytes 34816 | tf_op jit(solution)/shard_map/all_gather | solution.py:34
  640.2 19.9 %all-gather.4 = f32[16,4,128]{2,1,0:T(4,128)S(1)} all-gather(f32[1,4,128]{2,1,0:T(4,128)S(1)} %bitcast.76), channel_id=3, replica_groups=mesh['ctx'=16,'head'=8] {'ctx'}, dimensions={0}, use_global_device_ids=true | all-gather | bytes 34816 | tf_op jit(solution)/shard_map/all_gather | solution.py:34
  660.0 1.3 convolution_bitcast_fusion
  662.4 18.9 %while.19 = (s32[]{:T(128)}, f32[4,128]{1,0:T(4,128)S(1)}, f32[4,128]{1,0:T(4,128)S(1)}, f32[4,128,128]{2,1,0:T(8,128)S(1)}, f32[16,4,128]{2,1,0:T(4,128)S(1)}, ...) while((s32[]{:T(128)}, f32[4,128]{1,0:T(4,128)S(1)}, ...), condition=%wide.region_4.5_spmd, body=%wide.region_3.4_spmd.sunk | while | flops 199685 | bytes 807063 | solution.py:39
  662.4 1.2 fusion.61
  681.3 22.9 %copy.41 = bf16[16,1024,4,256]{3,1,0,2:T(8,128)(2,1)} copy(bf16[16,1024,4,256]{3,1,2,0:T(8,128)(2,1)} %all-to-all-done) | data formatting | bytes 67108864 | tf_op jit(solution)/shard_map/all_to_all | solution.py:81
  704.2 34.4 %fusion.11 = bf16[4,48,64,256]{3,1,2,0:T(8,128)(2,1)S(1)} fusion(bf16[256,64,4,256]{3,1,0,2:T(8,128)(2,1)} %bitcast.65, s32[4,48]{1,0:T(4,128)S(1)} %add.84), kind=kOutput, calls=%fused_computation.20 | convolution fusion | flops 1613807616 | bytes 39846656 | tf_op jit(solution)/shard_map/hrb,bthe->hrte/dot_general | solution.py:86
  738.5 2.5 copy.43
  741.0 1.8 fusion.55
  742.8 4.1 fusion.18
  746.9 28.1 %fusion.57 = (f32[16,4,64]{2,1,0:T(4,128)S(1)}, f32[16,4,64,512]{3,2,1,0:T(8,128)}) fusion(f32[16,4,64,192]{3,2,1,0:T(8,128)} %fusion.18, f32[16,4,64,128]{3,2,1,0:T(8,128)S(1)} %convolution_bitcast_fusion, f32[16,4,64,192]{3,2,1,0:T(8,128)S(1)} %copy-done.4), kind=kOutput, calls=%fused_computation.71 | output fusion | flops 10486271 | bytes 16793600 | tf_op jit(solution)/shard_map/sub | solution.py:113
  775.0 4.1 divide_convert_fusion
  779.0 1.3 fusion.14
  780.3 1.6 fusion.36
  782.3 1.4 fusion.29
  784.1 1.8 copy.49
  (67 shorter events, 22.0 us)
Async XLA Ops:
  6.5 97.4 %all-gather.8.cloned.1.call-start = ((), (), s32[]{:S(2)}) async-start(), calls=%async_computation.1 | async-start | bytes 9437184 | tf_op jit(solution)/shard_map/all_gather | solution.py:52
  122.3 1.7 copy-start.3
  135.1 546.1 %all-to-all-start = ((bf16[16,1024,4,256]{3,1,2,0:T(8,128)(2,1)}), bf16[16,1024,4,256]{3,1,2,0:T(8,128)(2,1)}, u32[]{:S(2)}, u32[]{:S(2)}) async-start(bf16[16,1024,4,256]{3,1,2,0:T(8,128)(2,1)} %stack.2), calls=%async_computation | async-start | bytes 67108864 | tf_op jit(solution)/shard_map/all_to_all | solution.py:81
  142.5 279.8 %all-reduce.2.cloned.1.call-start = ((), (), s32[]{:S(2)}) async-start(), calls=%async_computation.2 | async-start | bytes 786432 | tf_op jit(solution)/shard_map/psum | solution.py:30
  144.4 287.3 %copy-start.5 = (s32[4,256,3]{1,0,2:T(4,128)S(1)}, s32[4,256,3]{1,0,2:T(4,128)}, u32[]{:S(2)}) copy-start(s32[4,256,3]{1,0,2:T(4,128)} %param.9) | copy-start | bytes 36868
  144.4 287.3 %copy-start.6 = (s32[4,256,3]{1,0,2:T(4,128)S(1)}, s32[4,256,3]{1,0,2:T(4,128)}, u32[]{:S(2)}) copy-start(s32[4,256,3]{1,0,2:T(4,128)} %param.8) | copy-start | bytes 36868
  144.4 517.0 %all-gather.10.cloned.1.call-start = ((), (), s32[]{:S(2)}) async-start(), calls=%async_computation.3 | async-start | bytes 4456448 | tf_op jit(solution)/shard_map/all_gather | solution.py:34
  424.2 1.5 copy-start
  430.7 173.7 %collective-permute-start = (bf16[64,4,256]{2,0,1:T(8,128)(2,1)}, bf16[64,4,256]{2,0,1:T(8,128)(2,1)S(1)}, u32[]{:S(2)}, u32[]{:S(2)}) collective-permute-start(bf16[64,4,256]{2,0,1:T(8,128)(2,1)} %get-tuple-element.206), channel_id=1, source_target_pairs={{0,8},{8,16},{16,24},{24,32},{32,40},{40,48},{48,56},{56,64},{64,7... | collective-permute-start | bytes 393224 | tf_op jit(solution)/shard_map/ppermute | solution.py:19
  431.4 173.0 %collective-permute-start.1 = (bf16[64,4,256]{2,0,1:T(8,128)(2,1)S(1)}, bf16[64,4,256]{2,0,1:T(8,128)(2,1)S(1)}, u32[]{:S(2)}, u32[]{:S(2)}) collective-permute-start(bf16[64,4,256]{2,0,1:T(8,128)(2,1)S(1)} %get-tuple-element.207), channel_id=1, source_target_pairs={{8,0},{16,8},{24,16},{32,24},{40,32},{48,40},{56,48},{64,56},{72,6... | collective-permute-start | bytes 393224 | tf_op jit(solution)/shard_map/ppermute | solution.py:21
  613.1 26.5 %copy-start.1 = (f32[4,128,1024]{2,1,0:T(8,128)S(1)}, f32[4,128,1024]{2,1,0:T(8,128)}, u32[]{:S(2)}) copy-start(f32[4,128,1024]{2,1,0:T(8,128)} %copy-done) | copy-start | bytes 6291460
  742.8 4.1 copy-start.4
  780.3 2.0 copy-start.2
Sparse Core Ops, SparseCore 0:
  9.0 94.9 all-gather.7
  145.8 276.4 all-reduce.1
  429.2 158.1 all-gather.9
